TPU v7x, 32 devices: a whole 2x2x4 slice. The times are simulated.
32 devices in a mesh: gz: 8 (over z, y), gy: 4 (over x, core).
Axes of the slice: x: 2, y: 2, z: 4, core: 2. Of those that a mesh axis runs over, the one named last changes fastest.
Arguments:
- phase: float32 [32, 128, 768], P('gz', 'gy'), may hold values from 0 to 1
- solute: float32 [32, 128, 768], P('gz', 'gy'), may hold values from -0.5 to 0.5
- labels: int32 [32, 128, 768], P('gz', 'gy'), may hold values from 0 to 31
- quat_table: float32 [32, 4], replicated, may hold values from -3 to 3
- heat_map: float32 [128, 768], P('gy'), may hold values from -4 to 4
- cotangent: float32 [6, 32, 128, 768], P(None, 'gz', 'gy'), may hold values from -6 to 6
Outputs:
- final_fields: float32 [6, 32, 128, 768], P(None, 'gz', 'gy')
- sensitivity: float32 [128, 768], P('gy')
- objective: float32 [], replicated
All inputs are finite; a program needn't handle non-finite values.
Results may differ from a plain program's by a relative error of at most 0.0003.
Values sent between devices are 32-bit elements; how exact they have to be, the bound alone decides.
A program may use at most 128 MiB of HBM per device.

v0:
```python
import jax
import jax.numpy as jnp
from jax import lax
from jax.sharding import PartitionSpec as P

time_step = 0.08
drive_gain = 0.6
misfit_gain = 0.2
solute_diff = 0.8
reject_gain = 0.5
solute_shift = 0.5


def padded_2(cells, sides, width):
    for axis, dim in sides:
        count = lax.axis_size(axis)
        head = lax.slice_in_dim(cells, 0, width, axis=dim)
        tail = lax.slice_in_dim(cells, cells.shape[dim] - width, cells.shape[dim], axis=dim)
        cells = jnp.concatenate(
            [
                lax.ppermute(tail, axis, [(i, (i + 1) % count) for i in range(count)]),
                cells,
                lax.ppermute(head, axis, [((i + 1) % count, i) for i in range(count)]),
            ],
            axis=dim,
        )
    return cells


def advance(padded, heat_rows):
    center = padded[:, 1:-1, 1:-1, :]
    border = jnp.zeros_like(center[..., :1])
    laplace = (
        padded[:, 2:, 1:-1, :]
        + padded[:, :-2, 1:-1, :]
        + padded[:, 1:-1, 2:, :]
        + padded[:, 1:-1, :-2, :]
        + jnp.concatenate([center[..., 1:], border], -1)
        + jnp.concatenate([border, center[..., :-1]], -1)
        - 6.0 * center
    )
    phase_now = center[0]
    quaternions = center[1:5]
    solute_now = center[5]
    undercool = heat_rows[None] - solute_shift * solute_now
    misfit = jnp.sum(quaternions * laplace[1:5], axis=0)
    phase_next = phase_now + time_step * (
        laplace[0]
        + 4.0 * phase_now * (1.0 - phase_now) * (phase_now - 0.5 + drive_gain * jnp.tanh(undercool))
        + misfit_gain * phase_now * misfit
    )
    quat_next = quaternions + time_step * ((1.0 - phase_now) ** 2 + 0.1) * laplace[1:5]
    solute_next = (
        solute_now
        + time_step * solute_diff * laplace[5]
        + reject_gain * (phase_next - phase_now) * solute_now
    )
    return jnp.concatenate([phase_next[None], quat_next, solute_next[None]], 0)


def expand_labels(grain_ids, quat_table):
    total = jnp.zeros((4,) + grain_ids.shape, jnp.float32)
    for grain in range(quat_table.shape[0]):
        total = total + jnp.where(
            grain_ids[None] == grain, quat_table[grain][:, None, None, None], 0.0
        )
    return total


def clear_rows(padded, width, low_edge, high_edge):
    rows = jnp.arange(padded.shape[2])
    dropped = (rows < width) & low_edge | (rows >= padded.shape[2] - width) & high_edge
    return jnp.where(dropped[None, None, :, None], 0.0, padded)


def cycle_total(partial_value):
    return lax.psum(partial_value, "gz")


def on_device(phase, solute, labels, quat_table, heat_map, cotangent):
    gy_index = lax.axis_index("gy")
    low_edge = gy_index == 0
    high_edge = gy_index == lax.axis_size("gy") - 1
    stored = []
    fields_first = jnp.concatenate(
        [phase[None], expand_labels(labels, quat_table), solute[None]], 0
    )
    padded = clear_rows(padded_2(fields_first, (("gz", 1), ("gy", 2)), 1), 1, low_edge, high_edge)
    stored.append(padded)
    fields_now = advance(padded, heat_map)
    padded = clear_rows(padded_2(fields_now, (("gz", 1), ("gy", 2)), 1), 1, low_edge, high_edge)
    stored.append(padded)
    fields_now = advance(padded, heat_map)
    objective = lax.psum(jnp.sum(cotangent * fields_now), ("gz", "gy"))
    last_pull = jax.vjp(advance, stored[1], heat_map)[1]
    grad_padded, grad_map_late = last_pull(cotangent)
    summed_late = cycle_total(grad_map_late)
    received = padded_2(grad_padded, (("gz", 1), ("gy", 2)), 1)
    low_keep = jnp.where(low_edge, 0.0, 1.0)
    high_keep = jnp.where(high_edge, 0.0, 1.0)
    adjoint = grad_padded[:, 1:-1, 1:-1, :]
    adjoint = adjoint.at[:, 0].add(received[:, 0, 2:-2, :])
    adjoint = adjoint.at[:, -1].add(received[:, -1, 2:-2, :])
    adjoint = adjoint.at[:, :, 0].add(low_keep * received[:, 2:-2, 0, :])
    adjoint = adjoint.at[:, :, -1].add(high_keep * received[:, 2:-2, -1, :])
    first_stored = stored[0]
    first_pull = jax.vjp(lambda heat: advance(first_stored, heat), heat_map)[1]
    grad_map_early = first_pull(adjoint)[0]
    sensitivity = summed_late + cycle_total(grad_map_early)
    return (fields_now, sensitivity, objective)


def solution(mesh):
    placed = (
        P("gz", "gy", None),
        P("gz", "gy", None),
        P("gz", "gy", None),
        P(),
        P("gy", None),
        P(None, "gz", "gy", None),
    )
    return jax.shard_map(
        on_device,
        mesh=mesh,
        in_specs=placed,
        out_specs=(P(None, "gz", "gy", None), P("gy", None), P()),
        check_vma=False,
    )
```

profile of v0, /device:TPU:0, one launch (start us, length us, event | category | flops | bytes accessed | tf_op | source)
XLA Modules:
  0.0 244.5 jit_solution(5796627415855076050)
XLA Ops:
  7.2 1.9 slice_reduce_fusion.31
  9.1 1.6 slice_reduce_fusion.30
  10.7 3.4 %broadcast_compare_fusion.31 = (pred[4,32,768]{2,1,0:T(8,128)(4,1)S(1)}, pred[4,32,768]{2,1,0:T(8,128)(4,1)S(1)}, pred[4,32,768]{2,1,0:T(8,128)(4,1)S(1)}, pred[...) fusion(s32[4,32,768]{2,1,0:T(8,128)} %param.16), kind=kLoop, calls=%fused_computation.127 | loop fusion | flops 3145728 | bytes 3538944 | tf_op jit(solution)/shard_map/eq | solution.py:65
  14.1 5.4 %select_add_fusion = f32[4,4,32,768]{3,2,1,0:T(8,128)S(1)} fusion(f32[4]{0:T(128)S(1)} %get-tuple-element.88, f32[4]{0:T(128)S(1)} %get-tuple-element.89, f32[4]{0:T(128)S(1)} %get-tuple-element.59, f32[4]{0:T(128)S(1)} %get-tuple-element.60, f32[4]{0:T(128)S(1)} %get-tuple-element.61, f32[4]{0:T(128)S(1)} %get-tuple-element.62, f32[4]{0:T(128)S(1)} %get-tuple-element.63, ...), kind=kLoop, calls=%fused_computation.27 | loop fusion | flops 24772608 | bytes 4719104 | tf_op jit(solution)/shard_map/add | solution.py:64
  19.5 1.1 pad_maximum_fusion.6
  20.6 3.0 %collective-permute-start = (f32[6,1,32,768]{3,2,1,0:T(8,128)}, f32[6,1,32,768]{3,2,1,0:T(8,128)S(1)}, u32[]{:S(2)}, u32[]{:S(2)}) collective-permute-start(f32[6,1,32,768]{3,2,1,0:T(8,128)} %get-tuple-element.121), channel_id=1, source_target_pairs={{0,4},{4,8},{8,12},{12,16},{16,20},{20,24},{24,28},{28,0},{1,5},{5... | collective-permute-start | bytes 1769480 | tf_op jit(solution)/shard_map/ppermute | solution.py:21
  23.6 3.0 %collective-permute-start.1 = (f32[6,1,32,768]{3,2,1,0:T(8,128)}, f32[6,1,32,768]{3,2,1,0:T(8,128)S(1)}, u32[]{:S(2)}, u32[]{:S(2)}) collective-permute-start(f32[6,1,32,768]{3,2,1,0:T(8,128)} %get-tuple-element.122), channel_id=1, source_target_pairs={{4,0},{8,4},{12,8},{16,12},{20,16},{24,20},{28,24},{0,28},{5,1},{9... | collective-permute-start | bytes 1769480 | tf_op jit(solution)/shard_map/ppermute | solution.py:23
  26.6 22.5 %collective-permute-done = f32[6,1,32,768]{3,2,1,0:T(8,128)S(1)} collective-permute-done((f32[6,1,32,768]{3,2,1,0:T(8,128)}, f32[6,1,32,768]{3,2,1,0:T(8,128)S(1)}, u32[]{:S(2)}, u32[]{:S(2)}) %collective-permute-start) | collective-permute-done | bytes 589856 | tf_op jit(solution)/shard_map/ppermute | solution.py:21
  49.1 2.1 collective-permute-done.1
  51.2 0.2 pad_maximum_fusion.19
  51.5 1.7 collective-permute-start.3
  53.2 2.4 collective-permute-done.2
  55.6 0.2 collective-permute-done.3
  55.8 1.0 maximum_select_fusion
  56.9 1.1 fusion.45
  58.1 1.3 fusion.3
  59.4 0.4 multiply_add_fusion.2
  59.8 0.5 copy-done.8
  60.3 0.3 fusion.23
  60.7 0.3 collective-permute-start.4
  61.0 4.4 %collective-permute-start.5 = (f32[6,1,32,768]{3,2,1,0:T(8,128)S(1)}, f32[6,1,32,768]{3,2,1,0:T(8,128)S(1)}, u32[]{:S(2)}, u32[]{:S(2)}) collective-permute-start(f32[6,1,32,768]{3,2,1,0:T(8,128)S(1)} %get-tuple-element.120), channel_id=1, source_target_pairs={{4,0},{8,4},{12,8},{16,12},{20,16},{24,20},{28,24},{0,28},{5,1},{9... | collective-permute-start | bytes 1769480 | tf_op jit(solution)/shard_map/ppermute | solution.py:23
  65.5 21.6 %collective-permute-done.4 = f32[6,1,32,768]{3,2,1,0:T(8,128)S(1)} collective-permute-done((f32[6,1,32,768]{3,2,1,0:T(8,128)S(1)}, f32[6,1,32,768]{3,2,1,0:T(8,128)S(1)}, u32[]{:S(2)}, u32[]{:S(2)}) %collective-permute-start.4) | collective-permute-done | bytes 589856 | tf_op jit(solution)/shard_map/ppermute | solution.py:21
  87.0 2.9 %collective-permute-done.5 = f32[6,1,32,768]{3,2,1,0:T(8,128)S(1)} collective-permute-done((f32[6,1,32,768]{3,2,1,0:T(8,128)S(1)}, f32[6,1,32,768]{3,2,1,0:T(8,128)S(1)}, u32[]{:S(2)}, u32[]{:S(2)}) %collective-permute-start.5) | collective-permute-done | bytes 589856 | tf_op jit(solution)/shard_map/ppermute | solution.py:23
  89.9 0.2 pad_maximum_fusion.14
  90.1 0.2 collective-permute-start.6
  90.3 1.6 collective-permute-start.7
  91.9 2.4 collective-permute-done.6
  94.3 0.4 collective-permute-done.7
  94.7 1.0 maximum_select_fusion.1
  95.7 2.9 %fusion.44 = (f32[6,4,32,767]{3,2,1,0:T(8,128)S(1)}, f32[6,4,32,767]{3,2,1,0:T(8,128)}) fusion(f32[6,6,34,768]{3,2,1,0:T(8,128)S(1)} %maximum_select_fusion.1), kind=kLoop, calls=%fused_computation.179 | loop fusion | bytes 9424896 | tf_op jit(solution)/shard_map/slice | solution.py:38
  98.7 3.1 %fusion = f32[6,4,32,768]{3,2,1,0:T(8,128)S(1)} fusion(f32[6,6,34,768]{3,2,1,0:T(8,128)S(1)} %maximum_select_fusion.1, f32[6,4,32,767]{3,2,1,0:T(8,128)} %get-tuple-element.108, f32[6,4,32,767]{3,2,1,0:T(8,128)S(1)} %get-tuple-element.107), kind=kLoop, calls=%fused_computation.4 | loop fusion | flops 4128768 | bytes 18868224 | tf_op jit(solution)/shard_map/sub | solution.py:34
  101.8 1.8 multiply_reduce_fusion.1
  103.5 0.5 fusion.8
  104.0 0.4 copy-done.9
  104.4 0.6 fusion.34
  105.0 0.4 multiply_add_fusion
  105.4 0.3 pad_add_fusion.2
  105.7 0.8 fusion.46
  106.6 1.2 pad_add_fusion.1
  107.8 1.7 pad_add_fusion
  109.5 2.1 copy-done.2
  111.6 1.2 fusion.43
  112.8 4.7 %collective-permute-start.9 = (f32[6,1,34,768]{3,2,1,0:T(8,128)}, f32[6,1,34,768]{3,2,1,0:T(8,128)}, u32[]{:S(2)}, u32[]{:S(2)}) collective-permute-start(f32[6,1,34,768]{3,2,1,0:T(8,128)} %get-tuple-element.104), channel_id=1, source_target_pairs={{4,0},{8,4},{12,8},{16,12},{20,16},{24,20},{28,24},{0,28},{5,1},{9... | collective-permute-start | bytes 1880072 | tf_op jit(solution)/shard_map/ppermute | solution.py:23
  117.5 2.2 slice.467
  119.8 25.3 %collective-permute-done.8 = f32[6,1,34,768]{3,2,1,0:T(8,128)} collective-permute-done((f32[6,1,34,768]{3,2,1,0:T(8,128)}, f32[6,1,34,768]{3,2,1,0:T(8,128)}, u32[]{:S(2)}, u32[]{:S(2)}) %collective-permute-start.8) | collective-permute-done | bytes 626720 | tf_op jit(solution)/shard_map/ppermute | solution.py:21
  145.1 3.7 %collective-permute-done.9 = f32[6,1,34,768]{3,2,1,0:T(8,128)} collective-permute-done((f32[6,1,34,768]{3,2,1,0:T(8,128)}, f32[6,1,34,768]{3,2,1,0:T(8,128)}, u32[]{:S(2)}, u32[]{:S(2)}) %collective-permute-start.9) | collective-permute-done | bytes 626720 | tf_op jit(solution)/shard_map/ppermute | solution.py:23
  148.8 1.4 pad_maximum_fusion.7
  150.2 0.2 collective-permute-start.10
  150.5 0.7 copy.50
  151.1 1.6 collective-permute-start.11
  152.7 1.3 fusion.7
  154.0 1.3 fusion.6
  155.3 1.4 copy-done.5
  156.7 0.7 slice_add_fusion.12
  157.4 2.1 scatter-add.16
  159.4 0.9 slice.477
  160.4 1.8 slice_add_fusion.11
  162.2 2.1 scatter-add.19
  164.3 2.2 fusion.16
  166.5 0.7 add.362
  167.2 4.0 %multiply_reduce_fusion = (f32[]{:T(128)}, f32[6,4,32,768]{3,2,1,0:T(8,128)}) fusion(f32[6,4,32,768]{3,2,1,0:T(8,128)S(1)} %copy-done.4, f32[1,4,32,768]{3,2,1,0:T(8,128)S(1)} %get-tuple-element.106, f32[4,4,32,768]{3,2,1,0:T(8,128)} %get-tuple-element.97, f32[1,4,32,768]{3,2,1,0:T(8,128)S(1)} %get-tuple-element.94), kind=kLoop, calls=%fused_computation.18 | loop fusion | flops 2359295 | bytes 7077892 | tf_op jit(solution)/shard_map/reduce_sum | solution.py:94
  171.2 39.7 %psum.23 = f32[]{:T(128)} all-reduce(f32[]{:T(128)} %get-tuple-element.90), channel_id=1, replica_groups=mesh['gz'=8,'gy'=4] {'gz','gy'}, use_global_device_ids=true, to_apply=%region_8.9 | all-reduce | flops 1 | bytes 8 | tf_op jit(solution)/shard_map/psum | solution.py:94
  210.9 25.2 %all-reduce.20.cloned.1.call-done = f32[32,768]{1,0:T(8,128)} async-done(((f32[32,768]{1,0:T(8,128)}), f32[32,768]{1,0:T(8,128)}) %all-reduce.20.cloned.1.call-update) | async-done | bytes 98320 | tf_op jit(solution)/shard_map/psum | solution.py:77
  236.1 1.5 copy.65
  (28 shorter events, 0.4 us)
Async XLA Ops:
  7.2 228.9 %all-reduce.20.cloned.1.call-start = ((), (), s32[]{:S(2)}) async-start(), calls=%async_computation | async-start | bytes 196608 | tf_op jit(solution)/shard_map/psum | solution.py:77
  14.1 5.4 %copy-start.6 = (f32[4,32,768]{2,1,0:T(8,128)S(1)}, f32[4,32,768]{2,1,0:T(8,128)}, u32[]{:S(2)}) copy-start(f32[4,32,768]{2,1,0:T(8,128)} %param.15) | copy-start | bytes 1179652
  14.1 5.4 %copy-start.7 = (f32[4,32,768]{2,1,0:T(8,128)S(1)}, f32[4,32,768]{2,1,0:T(8,128)}, u32[]{:S(2)}) copy-start(f32[4,32,768]{2,1,0:T(8,128)} %param.14) | copy-start | bytes 1179652
  20.6 28.5 %collective-permute-start = (f32[6,1,32,768]{3,2,1,0:T(8,128)}, f32[6,1,32,768]{3,2,1,0:T(8,128)S(1)}, u32[]{:S(2)}, u32[]{:S(2)}) collective-permute-start(f32[6,1,32,768]{3,2,1,0:T(8,128)} %get-tuple-element.121), channel_id=1, source_target_pairs={{0,4},{4,8},{8,12},{12,16},{16,20},{20,24},{24,28},{28,0},{1,5},{5... | collective-permute-start | bytes 1769480 | tf_op jit(solution)/shard_map/ppermute | solution.py:21
  23.6 27.6 %collective-permute-start.1 = (f32[6,1,32,768]{3,2,1,0:T(8,128)}, f32[6,1,32,768]{3,2,1,0:T(8,128)S(1)}, u32[]{:S(2)}, u32[]{:S(2)}) collective-permute-start(f32[6,1,32,768]{3,2,1,0:T(8,128)} %get-tuple-element.122), channel_id=1, source_target_pairs={{4,0},{8,4},{12,8},{16,12},{20,16},{24,20},{28,24},{0,28},{5,1},{9... | collective-permute-start | bytes 1769480 | tf_op jit(solution)/shard_map/ppermute | solution.py:23
  51.4 4.2 %collective-permute-start.2 = (f32[6,6,1,768]{3,2,1,0:T(1,128)S(1)}, f32[6,6,1,768]{3,2,1,0:T(1,128)S(1)}, u32[]{:S(2)}, u32[]{:S(2)}) collective-permute-start(f32[6,6,1,768]{3,2,1,0:T(1,128)S(1)} %get-tuple-element.113), channel_id=1, source_target_pairs={{0,1},{1,2},{2,3},{3,0},{4,5},{5,6},{6,7},{7,4},{8,9},{9,10},{10,1... | collective-permute-start | bytes 331784 | tf_op jit(solution)/shard_map/ppermute | solution.py:21
  51.5 4.4 %collective-permute-start.3 = (f32[6,6,1,768]{3,2,1,0:T(1,128)S(1)}, f32[6,6,1,768]{3,2,1,0:T(1,128)S(1)}, u32[]{:S(2)}, u32[]{:S(2)}) collective-permute-start(f32[6,6,1,768]{3,2,1,0:T(1,128)S(1)} %get-tuple-element.114), channel_id=1, source_target_pairs={{1,0},{2,1},{3,2},{0,3},{5,4},{6,5},{7,6},{4,7},{9,8},{10,9},{11,1... | collective-permute-start | bytes 331784 | tf_op jit(solution)/shard_map/ppermute | solution.py:23
  56.9 2.9 %copy-start.1 = (f32[6,6,34,768]{3,2,1,0:T(8,128)}, f32[6,6,34,768]{3,2,1,0:T(8,128)S(1)}, u32[]{:S(2)}) copy-start(f32[6,6,34,768]{3,2,1,0:T(8,128)S(1)} %maximum_select_fusion) | copy-start | bytes 11280388
  59.4 0.9 copy-start.8
  60.7 26.3 %collective-permute-start.4 = (f32[6,1,32,768]{3,2,1,0:T(8,128)S(1)}, f32[6,1,32,768]{3,2,1,0:T(8,128)S(1)}, u32[]{:S(2)}, u32[]{:S(2)}) collective-permute-start(f32[6,1,32,768]{3,2,1,0:T(8,128)S(1)} %get-tuple-element.119), channel_id=1, source_target_pairs={{0,4},{4,8},{8,12},{12,16},{16,20},{20,24},{24,28},{28,0},{1,5},{5... | collective-permute-start | bytes 1769480 | tf_op jit(solution)/shard_map/ppermute | solution.py:21
  61.0 28.9 %collective-permute-start.5 = (f32[6,1,32,768]{3,2,1,0:T(8,128)S(1)}, f32[6,1,32,768]{3,2,1,0:T(8,128)S(1)}, u32[]{:S(2)}, u32[]{:S(2)}) collective-permute-start(f32[6,1,32,768]{3,2,1,0:T(8,128)S(1)} %get-tuple-element.120), channel_id=1, source_target_pairs={{4,0},{8,4},{12,8},{16,12},{20,16},{24,20},{28,24},{0,28},{5,1},{9... | collective-permute-start | bytes 1769480 | tf_op jit(solution)/shard_map/ppermute | solution.py:23
  90.1 4.2 %collective-permute-start.6 = (f32[6,6,1,768]{3,2,1,0:T(1,128)S(1)}, f32[6,6,1,768]{3,2,1,0:T(1,128)S(1)}, u32[]{:S(2)}, u32[]{:S(2)}) collective-permute-start(f32[6,6,1,768]{3,2,1,0:T(1,128)S(1)} %get-tuple-element.111), channel_id=1, source_target_pairs={{0,1},{1,2},{2,3},{3,0},{4,5},{5,6},{6,7},{7,4},{8,9},{9,10},{10,1... | collective-permute-start | bytes 331784 | tf_op jit(solution)/shard_map/ppermute | solution.py:21
  90.3 4.4 %collective-permute-start.7 = (f32[6,6,1,768]{3,2,1,0:T(1,128)S(1)}, f32[6,6,1,768]{3,2,1,0:T(1,128)S(1)}, u32[]{:S(2)}, u32[]{:S(2)}) collective-permute-start(f32[6,6,1,768]{3,2,1,0:T(1,128)S(1)} %get-tuple-element.112), channel_id=1, source_target_pairs={{1,0},{2,1},{3,2},{0,3},{5,4},{6,5},{7,6},{4,7},{9,8},{10,9},{11,1... | collective-permute-start | bytes 331784 | tf_op jit(solution)/shard_map/ppermute | solution.py:23
  95.7 9.3 %copy-start = (f32[6,6,34,768]{3,2,1,0:T(8,128)}, f32[6,6,34,768]{3,2,1,0:T(8,128)S(1)}, u32[]{:S(2)}) copy-start(f32[6,6,34,768]{3,2,1,0:T(8,128)S(1)} %maximum_select_fusion.1) | copy-start | bytes 11280388
  98.7 3.1 %copy-start.4 = (f32[6,4,32,768]{3,2,1,0:T(8,128)S(1)}, f32[6,4,32,768]{3,2,1,0:T(8,128)}, u32[]{:S(2)}) copy-start(f32[6,4,32,768]{3,2,1,0:T(8,128)} %param.19) | copy-start | bytes 7077892
  103.5 0.9 copy-start.9
  109.5 2.1 copy-start.2
  112.8 32.3 %collective-permute-start.8 = (f32[6,1,34,768]{3,2,1,0:T(8,128)}, f32[6,1,34,768]{3,2,1,0:T(8,128)}, u32[]{:S(2)}, u32[]{:S(2)}) collective-permute-start(f32[6,1,34,768]{3,2,1,0:T(8,128)} %get-tuple-element.105), channel_id=1, source_target_pairs={{0,4},{4,8},{8,12},{12,16},{16,20},{20,24},{24,28},{28,0},{1,5},{5... | collective-permute-start | bytes 1880072 | tf_op jit(solution)/shard_map/ppermute | solution.py:21
  112.8 36.0 %collective-permute-start.9 = (f32[6,1,34,768]{3,2,1,0:T(8,128)}, f32[6,1,34,768]{3,2,1,0:T(8,128)}, u32[]{:S(2)}, u32[]{:S(2)}) collective-permute-start(f32[6,1,34,768]{3,2,1,0:T(8,128)} %get-tuple-element.104), channel_id=1, source_target_pairs={{4,0},{8,4},{12,8},{16,12},{20,16},{24,20},{28,24},{0,28},{5,1},{9... | collective-permute-start | bytes 1880072 | tf_op jit(solution)/shard_map/ppermute | solution.py:23
  117.5 31.3 %copy-start.3 = (f32[6,6,34,768]{3,2,1,0:T(8,128)S(1)}, f32[6,6,34,768]{3,2,1,0:T(8,128)}, u32[]{:S(2)}) copy-start(f32[6,6,34,768]{3,2,1,0:T(8,128)} %copy-done.2) | copy-start | bytes 11280388
  150.2 5.0 %collective-permute-start.10 = (f32[6,8,1,768]{3,1,2,0:T(8,128)S(1)}, f32[6,8,1,768]{3,1,2,0:T(8,128)S(1)}, u32[]{:S(2)}, u32[]{:S(2)}) collective-permute-start(f32[6,8,1,768]{3,1,2,0:T(8,128)S(1)} %copy.48), channel_id=1, source_target_pairs={{0,1},{1,2},{2,3},{3,0},{4,5},{5,6},{6,7},{7,4},{8,9},{9,10},{10,1... | collective-permute-start | bytes 442376 | tf_op jit(solution)/shard_map/ppermute | solution.py:21
  151.1 8.3 %collective-permute-start.11 = (f32[6,8,1,768]{3,1,2,0:T(8,128)}, f32[6,8,1,768]{3,1,2,0:T(8,128)}, u32[]{:S(2)}, u32[]{:S(2)}) collective-permute-start(f32[6,8,1,768]{3,1,2,0:T(8,128)} %copy.50), channel_id=1, source_target_pairs={{1,0},{2,1},{3,2},{0,3},{5,4},{6,5},{7,6},{4,7},{9,8},{10,9},{11,1... | collective-permute-start | bytes 442376 | tf_op jit(solution)/shard_map/ppermute | solution.py:23
  155.2 1.4 copy-start.5
Sparse Core Ops, SparseCore 0:
  167.3 68.7 all-reduce.19
where the time goes:
time: 245 us; the launch traced here: 244 us
  waiting for transfers between devices  109 us (44%)
  blocking collectives  39.7 us (16%)
  other arithmetic  37.4 us (15%)
  local copies, waits for them, and re-layouts  23.4 us (10%)
  starting transfers between devices  20.9 us (9%)
  between operations  14.3 us (6%)
    ppermute x6, waiting for transfers between devices, padded_2(): lax.ppermute(tail, axis, [(i, (i + 1) % count) for i in range(count)])  74.2 us
    psum x1, blocking collectives, on_device(): objective = lax.psum(jnp.sum(cotangent * fields_now), ('gz', 'gy'))  39.7 us
    psum x1, waiting for transfers between devices, cycle_total(): return lax.psum(partial_value, 'gz')  25.2 us
    ppermute x6, starting transfers between devices, padded_2(): lax.ppermute(head, axis, [((i + 1) % count, i) for i in range(count)])  17.1 us
    ppermute x6, waiting for transfers between devices, padded_2(): lax.ppermute(head, axis, [((i + 1) % count, i) for i in range(count)])  9.27 us
    unnamed x21, local copies, waits for them, and re-layouts  5.95 us
    add x1, other arithmetic, expand_labels(): total + jnp.where(grain_ids[None] == grain, quat_table[grain][:, None, No...  5.4 us
  transfers between devices with their start and end apart: 13, of which 11 were waited for; matrix products, arithmetic and copies ran while one was open for 5% of the time, Pallas kernels for 0%

commit v1 on v0

--- a/solution.py
+++ b/solution.py
@@ -74,7 +74,7 @@
 
 
 def cycle_total(partial_value):
-    return lax.psum(partial_value, "gz")
+    return jnp.sum(lax.all_gather(partial_value, "gz"), axis=0)
 
 
 def on_device(phase, solute, labels, quat_table, heat_map, cotangent):

time: 245 us -> 255 us (1.041)
  blocking collectives: 39.7 us -> 125 us
  waiting for transfers between devices: 109 us -> 55.3 us
  between operations: 14.3 us -> 0.96 us
  local copies, waits for them, and re-layouts: 23.4 us -> 16.9 us
    all_gather x0 -> x2, blocking collectives: none -> 64.5 us  [cycle_total(): return jnp.sum(lax.all_gather(partial_value, 'gz'), axis=0)]
    psum x1 -> x0, waiting for transfers between devices: 25.2 us -> none  [cycle_total(): return lax.psum(partial_value, 'gz')]
    ppermute x6, waiting for transfers between devices: 74.2 us -> 49.1 us  [padded_2(): lax.ppermute(tail, axis, [(i, (i + 1) % count) for i in range(count)])]
    psum x1, blocking collectives: 39.7 us -> 60.7 us  [on_device(): objective = lax.psum(jnp.sum(cotangent * fields_now), ('gz', 'gy'))]
    ppermute x6, waiting for transfers between devices: 9.27 us -> 6.2 us  [padded_2(): lax.ppermute(head, axis, [((i + 1) % count, i) for i in range(count)])]
    unnamed x21 -> x20, local copies, waits for them, and re-layouts: 5.95 us -> 3.86 us
  transfers between devices with their start and end apart: 13 -> 12, of which waited for: 11 -> 10; matrix products, arithmetic and copies ran while one was open for 5% -> 4% of each run, Pallas kernels for 0% -> 0%
where the time goes in v1:
time: 255 us; the launch traced here: 254 us
  blocking collectives  125 us (49%)
  waiting for transfers between devices  55.3 us (22%)
  other arithmetic  34.9 us (14%)
  starting transfers between devices  21.1 us (8%)
  local copies, waits for them, and re-layouts  16.9 us (7%)
    all_gather x2, blocking collectives, cycle_total(): return jnp.sum(lax.all_gather(partial_value, 'gz'), axis=0)  64.5 us
    psum x1, blocking collectives, on_device(): objective = lax.psum(jnp.sum(cotangent * fields_now), ('gz', 'gy'))  60.7 us
    ppermute x6, waiting for transfers between devices, padded_2(): lax.ppermute(tail, axis, [(i, (i + 1) % count) for i in range(count)])  49.1 us
    ppermute x6, starting transfers between devices, padded_2(): lax.ppermute(head, axis, [((i + 1) % count, i) for i in range(count)])  17.3 us
    ppermute x6, waiting for transfers between devices, padded_2(): lax.ppermute(head, axis, [((i + 1) % count, i) for i in range(count)])  6.2 us
    add x1, other arithmetic, expand_labels(): total + jnp.where(grain_ids[None] == grain, quat_table[grain][:, None, No...  5.4 us
  transfers between devices with their start and end apart: 12, of which 10 were waited for; matrix products, arithmetic and copies ran while one was open for 4% of the time, Pallas kernels for 0%

profile of v1, /device:TPU:0, one launch (start us, length us, event | category | flops | bytes accessed | tf_op | source)
XLA Modules:
  0.0 254.3 jit_solution(2028934281545399394)
XLA Ops:
  0.6 1.9 slice_reduce_fusion.31
  2.5 1.6 slice_reduce_fusion.30
  4.1 3.4 %broadcast_compare_fusion.31 = (pred[4,32,768]{2,1,0:T(8,128)(4,1)S(1)}, pred[4,32,768]{2,1,0:T(8,128)(4,1)S(1)}, pred[4,32,768]{2,1,0:T(8,128)(4,1)S(1)}, pred[...) fusion(s32[4,32,768]{2,1,0:T(8,128)} %param.16), kind=kLoop, calls=%fused_computation.127 | loop fusion | flops 3145728 | bytes 3538944 | tf_op jit(solution)/shard_map/eq | solution.py:65
  7.5 5.4 %select_add_fusion = f32[4,4,32,768]{3,2,1,0:T(8,128)S(1)} fusion(f32[4]{0:T(128)S(1)} %get-tuple-element.88, f32[4]{0:T(128)S(1)} %get-tuple-element.89, f32[4]{0:T(128)S(1)} %get-tuple-element.59, f32[4]{0:T(128)S(1)} %get-tuple-element.60, f32[4]{0:T(128)S(1)} %get-tuple-element.61, f32[4]{0:T(128)S(1)} %get-tuple-element.62, f32[4]{0:T(128)S(1)} %get-tuple-element.63, ...), kind=kLoop, calls=%fused_computation.27 | loop fusion | flops 24772608 | bytes 4719104 | tf_op jit(solution)/shard_map/add | solution.py:64
  13.0 1.1 pad_maximum_fusion.6
  14.1 3.0 %collective-permute-start = (f32[6,1,32,768]{3,2,1,0:T(8,128)}, f32[6,1,32,768]{3,2,1,0:T(8,128)S(1)}, u32[]{:S(2)}, u32[]{:S(2)}) collective-permute-start(f32[6,1,32,768]{3,2,1,0:T(8,128)} %get-tuple-element.121), channel_id=1, source_target_pairs={{0,4},{4,8},{8,12},{12,16},{16,20},{20,24},{24,28},{28,0},{1,5},{5... | collective-permute-start | bytes 1769480 | tf_op jit(solution)/shard_map/ppermute | solution.py:21
  17.0 3.0 %collective-permute-start.1 = (f32[6,1,32,768]{3,2,1,0:T(8,128)}, f32[6,1,32,768]{3,2,1,0:T(8,128)S(1)}, u32[]{:S(2)}, u32[]{:S(2)}) collective-permute-start(f32[6,1,32,768]{3,2,1,0:T(8,128)} %get-tuple-element.122), channel_id=1, source_target_pairs={{4,0},{8,4},{12,8},{16,12},{20,16},{24,20},{28,24},{0,28},{5,1},{9... | collective-permute-start | bytes 1769480 | tf_op jit(solution)/shard_map/ppermute | solution.py:23
  20.1 22.5 %collective-permute-done = f32[6,1,32,768]{3,2,1,0:T(8,128)S(1)} collective-permute-done((f32[6,1,32,768]{3,2,1,0:T(8,128)}, f32[6,1,32,768]{3,2,1,0:T(8,128)S(1)}, u32[]{:S(2)}, u32[]{:S(2)}) %collective-permute-start) | collective-permute-done | bytes 589856 | tf_op jit(solution)/shard_map/ppermute | solution.py:21
  42.6 2.1 collective-permute-done.1
  44.7 0.2 pad_maximum_fusion.19
  44.9 1.7 collective-permute-start.3
  46.6 2.4 collective-permute-done.2
  49.0 0.2 collective-permute-done.3
  49.2 1.0 maximum_select_fusion
  50.3 1.1 fusion.45
  51.4 0.1 multiply_bitcast_fusion.2
  51.5 1.3 fusion.3
  52.8 0.4 multiply_add_fusion.2
  53.2 0.5 copy-done.7
  53.7 0.3 fusion.23
  54.0 0.1 pad_maximum_fusion.3
  54.1 0.3 collective-permute-start.4
  54.5 4.4 %collective-permute-start.5 = (f32[6,1,32,768]{3,2,1,0:T(8,128)S(1)}, f32[6,1,32,768]{3,2,1,0:T(8,128)S(1)}, u32[]{:S(2)}, u32[]{:S(2)}) collective-permute-start(f32[6,1,32,768]{3,2,1,0:T(8,128)S(1)} %get-tuple-element.120), channel_id=1, source_target_pairs={{4,0},{8,4},{12,8},{16,12},{20,16},{24,20},{28,24},{0,28},{5,1},{9... | collective-permute-start | bytes 1769480 | tf_op jit(solution)/shard_map/ppermute | solution.py:23
  58.9 21.6 %collective-permute-done.4 = f32[6,1,32,768]{3,2,1,0:T(8,128)S(1)} collective-permute-done((f32[6,1,32,768]{3,2,1,0:T(8,128)S(1)}, f32[6,1,32,768]{3,2,1,0:T(8,128)S(1)}, u32[]{:S(2)}, u32[]{:S(2)}) %collective-permute-start.4) | collective-permute-done | bytes 589856 | tf_op jit(solution)/shard_map/ppermute | solution.py:21
  80.5 2.9 %collective-permute-done.5 = f32[6,1,32,768]{3,2,1,0:T(8,128)S(1)} collective-permute-done((f32[6,1,32,768]{3,2,1,0:T(8,128)S(1)}, f32[6,1,32,768]{3,2,1,0:T(8,128)S(1)}, u32[]{:S(2)}, u32[]{:S(2)}) %collective-permute-start.5) | collective-permute-done | bytes 589856 | tf_op jit(solution)/shard_map/ppermute | solution.py:23
  83.3 0.2 pad_maximum_fusion.14
  83.5 0.4 collective-permute-start.6
  83.9 1.6 collective-permute-start.7
  85.5 2.4 collective-permute-done.6
  87.9 0.4 collective-permute-done.7
  88.3 1.0 maximum_select_fusion.1
  89.3 2.9 %fusion.44 = (f32[6,4,32,767]{3,2,1,0:T(8,128)S(1)}, f32[6,4,32,767]{3,2,1,0:T(8,128)}) fusion(f32[6,6,34,768]{3,2,1,0:T(8,128)S(1)} %maximum_select_fusion.1), kind=kLoop, calls=%fused_computation.179 | loop fusion | bytes 9424896 | tf_op jit(solution)/shard_map/slice | solution.py:38
  92.2 0.1 multiply_bitcast_fusion.1
  92.3 3.1 %fusion = f32[6,4,32,768]{3,2,1,0:T(8,128)S(1)} fusion(f32[6,6,34,768]{3,2,1,0:T(8,128)S(1)} %maximum_select_fusion.1, f32[6,4,32,767]{3,2,1,0:T(8,128)} %get-tuple-element.108, f32[6,4,32,767]{3,2,1,0:T(8,128)S(1)} %get-tuple-element.107), kind=kLoop, calls=%fused_computation.4 | loop fusion | flops 4128768 | bytes 18868224 | tf_op jit(solution)/shard_map/sub | solution.py:34
  95.4 1.8 multiply_reduce_fusion.1
  97.1 0.5 fusion.8
  97.6 0.4 copy-done.8
  98.0 0.6 fusion.34
  98.6 0.4 multiply_add_fusion
  99.0 0.3 pad_add_fusion.2
  99.3 0.8 fusion.46
  100.2 1.2 pad_add_fusion.1
  101.4 1.7 pad_add_fusion
  103.1 2.1 copy-done.2
  105.2 1.2 fusion.43
  106.4 4.7 %collective-permute-start.9 = (f32[6,1,34,768]{3,2,1,0:T(8,128)}, f32[6,1,34,768]{3,2,1,0:T(8,128)}, u32[]{:S(2)}, u32[]{:S(2)}) collective-permute-start(f32[6,1,34,768]{3,2,1,0:T(8,128)} %get-tuple-element.104), channel_id=1, source_target_pairs={{4,0},{8,4},{12,8},{16,12},{20,16},{24,20},{28,24},{0,28},{5,1},{9... | collective-permute-start | bytes 1880072 | tf_op jit(solution)/shard_map/ppermute | solution.py:23
  111.1 4.0 %multiply_reduce_fusion = (f32[]{:T(128)}, f32[6,4,32,768]{3,2,1,0:T(8,128)}) fusion(f32[6,4,32,768]{3,2,1,0:T(8,128)S(1)} %copy-done.4, f32[1,4,32,768]{3,2,1,0:T(8,128)S(1)} %get-tuple-element.106, f32[4,4,32,768]{3,2,1,0:T(8,128)} %get-tuple-element.97, f32[1,4,32,768]{3,2,1,0:T(8,128)S(1)} %get-tuple-element.94), kind=kLoop, calls=%fused_computation.18 | loop fusion | flops 2359295 | bytes 7077892 | tf_op jit(solution)/shard_map/reduce_sum | solution.py:94
  115.1 60.7 %psum.7 = f32[]{:T(128)} all-reduce(f32[]{:T(128)} %get-tuple-element.90), channel_id=1, replica_groups=mesh['gz'=8,'gy'=4] {'gz','gy'}, use_global_device_ids=true, to_apply=%region_8.9 | all-reduce | flops 1 | bytes 8 | tf_op jit(solution)/shard_map/psum | solution.py:94
  175.8 2.3 slice.467
  178.1 0.8 copy-done.3
  178.9 1.4 pad_maximum_fusion.7
  180.4 1.8 collective-permute-start.11
  182.2 1.3 fusion.7
  183.4 1.3 fusion.6
  184.7 0.2 collective-permute-done.10
  184.9 0.1 slice_add_fusion.12
  185.0 0.6 scatter-add.16
  185.7 0.6 collective-permute-done.11
  186.3 0.1 slice_add_fusion.11
  186.4 0.6 scatter-add.19
  187.1 2.0 fusion.16
  189.1 32.3 %all-gather = f32[256,768]{1,0:T(8,128)S(1)} all-gather(f32[32,768]{1,0:T(8,128)S(1)} %get-tuple-element.57), channel_id=2, replica_groups=mesh['gz'=8,'gy'=4] {'gz'}, dimensions={0}, use_global_device_ids=true | all-gather | bytes 884736 | tf_op jit(solution)/shard_map/all_gather | solution.py:77
  221.4 32.2 %all-gather.1 = f32[256,768]{1,0:T(8,128)S(1)} all-gather(f32[32,768]{1,0:T(8,128)S(1)} %get-tuple-element.56), channel_id=3, replica_groups=mesh['gz'=8,'gy'=4] {'gz'}, dimensions={0}, use_global_device_ids=true | all-gather | bytes 884736 | tf_op jit(solution)/shard_map/all_gather | solution.py:77
  253.6 0.7 add.358
  (28 shorter events, 0.3 us)
Async XLA Ops:
  7.5 5.4 %copy-start.5 = (f32[4,32,768]{2,1,0:T(8,128)S(1)}, f32[4,32,768]{2,1,0:T(8,128)}, u32[]{:S(2)}) copy-start(f32[4,32,768]{2,1,0:T(8,128)} %param.15) | copy-start | bytes 1179652
  7.5 5.4 %copy-start.6 = (f32[4,32,768]{2,1,0:T(8,128)S(1)}, f32[4,32,768]{2,1,0:T(8,128)}, u32[]{:S(2)}) copy-start(f32[4,32,768]{2,1,0:T(8,128)} %param.14) | copy-start | bytes 1179652
  14.1 28.5 %collective-permute-start = (f32[6,1,32,768]{3,2,1,0:T(8,128)}, f32[6,1,32,768]{3,2,1,0:T(8,128)S(1)}, u32[]{:S(2)}, u32[]{:S(2)}) collective-permute-start(f32[6,1,32,768]{3,2,1,0:T(8,128)} %get-tuple-element.121), channel_id=1, source_target_pairs={{0,4},{4,8},{8,12},{12,16},{16,20},{20,24},{24,28},{28,0},{1,5},{5... | collective-permute-start | bytes 1769480 | tf_op jit(solution)/shard_map/ppermute | solution.py:21
  17.0 27.6 %collective-permute-start.1 = (f32[6,1,32,768]{3,2,1,0:T(8,128)}, f32[6,1,32,768]{3,2,1,0:T(8,128)S(1)}, u32[]{:S(2)}, u32[]{:S(2)}) collective-permute-start(f32[6,1,32,768]{3,2,1,0:T(8,128)} %get-tuple-element.122), channel_id=1, source_target_pairs={{4,0},{8,4},{12,8},{16,12},{20,16},{24,20},{28,24},{0,28},{5,1},{9... | collective-permute-start | bytes 1769480 | tf_op jit(solution)/shard_map/ppermute | solution.py:23
  44.8 4.2 %collective-permute-start.2 = (f32[6,6,1,768]{3,2,1,0:T(1,128)S(1)}, f32[6,6,1,768]{3,2,1,0:T(1,128)S(1)}, u32[]{:S(2)}, u32[]{:S(2)}) collective-permute-start(f32[6,6,1,768]{3,2,1,0:T(1,128)S(1)} %get-tuple-element.113), channel_id=1, source_target_pairs={{0,1},{1,2},{2,3},{3,0},{4,5},{5,6},{6,7},{7,4},{8,9},{9,10},{10,1... | collective-permute-start | bytes 331784 | tf_op jit(solution)/shard_map/ppermute | solution.py:21
  44.9 4.4 %collective-permute-start.3 = (f32[6,6,1,768]{3,2,1,0:T(1,128)S(1)}, f32[6,6,1,768]{3,2,1,0:T(1,128)S(1)}, u32[]{:S(2)}, u32[]{:S(2)}) collective-permute-start(f32[6,6,1,768]{3,2,1,0:T(1,128)S(1)} %get-tuple-element.114), channel_id=1, source_target_pairs={{1,0},{2,1},{3,2},{0,3},{5,4},{6,5},{7,6},{4,7},{9,8},{10,9},{11,1... | collective-permute-start | bytes 331784 | tf_op jit(solution)/shard_map/ppermute | solution.py:23
  50.3 2.9 %copy-start.1 = (f32[6,6,34,768]{3,2,1,0:T(8,128)}, f32[6,6,34,768]{3,2,1,0:T(8,128)S(1)}, u32[]{:S(2)}) copy-start(f32[6,6,34,768]{3,2,1,0:T(8,128)S(1)} %maximum_select_fusion) | copy-start | bytes 11280388
  52.8 0.9 copy-start.7
  54.1 26.3 %collective-permute-start.4 = (f32[6,1,32,768]{3,2,1,0:T(8,128)S(1)}, f32[6,1,32,768]{3,2,1,0:T(8,128)S(1)}, u32[]{:S(2)}, u32[]{:S(2)}) collective-permute-start(f32[6,1,32,768]{3,2,1,0:T(8,128)S(1)} %get-tuple-element.119), channel_id=1, source_target_pairs={{0,4},{4,8},{8,12},{12,16},{16,20},{20,24},{24,28},{28,0},{1,5},{5... | collective-permute-start | bytes 1769480 | tf_op jit(solution)/shard_map/ppermute | solution.py:21
  54.5 28.9 %collective-permute-start.5 = (f32[6,1,32,768]{3,2,1,0:T(8,128)S(1)}, f32[6,1,32,768]{3,2,1,0:T(8,128)S(1)}, u32[]{:S(2)}, u32[]{:S(2)}) collective-permute-start(f32[6,1,32,768]{3,2,1,0:T(8,128)S(1)} %get-tuple-element.120), channel_id=1, source_target_pairs={{4,0},{8,4},{12,8},{16,12},{20,16},{24,20},{28,24},{0,28},{5,1},{9... | collective-permute-start | bytes 1769480 | tf_op jit(solution)/shard_map/ppermute | solution.py:23
  83.5 4.4 %collective-permute-start.6 = (f32[6,6,1,768]{3,2,1,0:T(1,128)S(1)}, f32[6,6,1,768]{3,2,1,0:T(1,128)S(1)}, u32[]{:S(2)}, u32[]{:S(2)}) collective-permute-start(f32[6,6,1,768]{3,2,1,0:T(1,128)S(1)} %get-tuple-element.111), channel_id=1, source_target_pairs={{0,1},{1,2},{2,3},{3,0},{4,5},{5,6},{6,7},{7,4},{8,9},{9,10},{10,1... | collective-permute-start | bytes 331784 | tf_op jit(solution)/shard_map/ppermute | solution.py:21
  83.9 4.4 %collective-permute-start.7 = (f32[6,6,1,768]{3,2,1,0:T(1,128)S(1)}, f32[6,6,1,768]{3,2,1,0:T(1,128)S(1)}, u32[]{:S(2)}, u32[]{:S(2)}) collective-permute-start(f32[6,6,1,768]{3,2,1,0:T(1,128)S(1)} %get-tuple-element.112), channel_id=1, source_target_pairs={{1,0},{2,1},{3,2},{0,3},{5,4},{6,5},{7,6},{4,7},{9,8},{10,9},{11,1... | collective-permute-start | bytes 331784 | tf_op jit(solution)/shard_map/ppermute | solution.py:23
  89.3 9.3 %copy-start = (f32[6,6,34,768]{3,2,1,0:T(8,128)}, f32[6,6,34,768]{3,2,1,0:T(8,128)S(1)}, u32[]{:S(2)}) copy-start(f32[6,6,34,768]{3,2,1,0:T(8,128)S(1)} %maximum_select_fusion.1) | copy-start | bytes 11280388
  92.3 3.1 %copy-start.4 = (f32[6,4,32,768]{3,2,1,0:T(8,128)S(1)}, f32[6,4,32,768]{3,2,1,0:T(8,128)}, u32[]{:S(2)}) copy-start(f32[6,4,32,768]{3,2,1,0:T(8,128)} %param.19) | copy-start | bytes 7077892
  97.1 0.9 copy-start.8
  103.1 2.1 copy-start.2
  106.4 71.7 %collective-permute-start.8 = (f32[6,1,34,768]{3,2,1,0:T(8,128)}, f32[6,1,34,768]{3,2,1,0:T(8,128)}, u32[]{:S(2)}, u32[]{:S(2)}) collective-permute-start(f32[6,1,34,768]{3,2,1,0:T(8,128)} %get-tuple-element.105), channel_id=1, source_target_pairs={{0,4},{4,8},{8,12},{12,16},{16,20},{20,24},{24,28},{28,0},{1,5},{5... | collective-permute-start | bytes 1880072 | tf_op jit(solution)/shard_map/ppermute | solution.py:21
  106.4 71.7 %collective-permute-start.9 = (f32[6,1,34,768]{3,2,1,0:T(8,128)}, f32[6,1,34,768]{3,2,1,0:T(8,128)}, u32[]{:S(2)}, u32[]{:S(2)}) collective-permute-start(f32[6,1,34,768]{3,2,1,0:T(8,128)} %get-tuple-element.104), channel_id=1, source_target_pairs={{4,0},{8,4},{12,8},{16,12},{20,16},{24,20},{28,24},{0,28},{5,1},{9... | collective-permute-start | bytes 1880072 | tf_op jit(solution)/shard_map/ppermute | solution.py:23
  175.8 3.1 %copy-start.3 = (f32[6,6,34,768]{3,2,1,0:T(8,128)S(1)}, f32[6,6,34,768]{3,2,1,0:T(8,128)}, u32[]{:S(2)}) copy-start(f32[6,6,34,768]{3,2,1,0:T(8,128)} %copy-done.2) | copy-start | bytes 11280388
  180.3 4.6 %collective-permute-start.10 = (f32[6,8,1,768]{3,1,2,0:T(8,128)S(1)}, f32[6,8,1,768]{3,1,2,0:T(8,128)S(1)}, u32[]{:S(2)}, u32[]{:S(2)}) collective-permute-start(f32[6,8,1,768]{3,1,2,0:T(8,128)S(1)} %copy.52), channel_id=1, source_target_pairs={{0,1},{1,2},{2,3},{3,0},{4,5},{5,6},{6,7},{7,4},{8,9},{9,10},{10,1... | collective-permute-start | bytes 442376 | tf_op jit(solution)/shard_map/ppermute | solution.py:21
  180.4 6.7 %copy-start.9 = (f32[32,768]{1,0:T(8,128)S(1)}, f32[32,768]{1,0:T(8,128)}, u32[]{:S(2)}) copy-start(f32[32,768]{1,0:T(8,128)} %param.18) | copy-start | bytes 294916
  180.4 5.9 %collective-permute-start.11 = (f32[6,8,1,768]{3,1,2,0:T(8,128)S(1)}, f32[6,8,1,768]{3,1,2,0:T(8,128)S(1)}, u32[]{:S(2)}, u32[]{:S(2)}) collective-permute-start(f32[6,8,1,768]{3,1,2,0:T(8,128)S(1)} %copy.54), channel_id=1, source_target_pairs={{1,0},{2,1},{3,2},{0,3},{5,4},{6,5},{7,6},{4,7},{9,8},{10,9},{11,1... | collective-permute-start | bytes 442376 | tf_op jit(solution)/shard_map/ppermute | solution.py:23
